TPU v7x, 32 devices: a whole 2x2x4 slice. The times are simulated.
32 devices in a mesh: hour: 16 (over z, y, x), region: 2 (over core).
Axes of the slice: x: 2, y: 2, z: 4, core: 2. Of those that a mesh axis runs over, the one named last changes fastest.
Arguments:
- demand: float32 [2240, 1024], P('hour', 'region'), may hold values from 0.2 to 2
- avail_factor: bfloat16 [2240, 8, 1024], P('hour', None, 'region'), may hold values from 0 to 1
- tech_mask: int32 [8, 1024], P(None, 'region'), may hold values 0 or 1
- var_cost: float32 [8, 1024], P(None, 'region'), may hold values from 0.1 to 2
- inv_cost: float32 [8, 1024], P(None, 'region'), may hold values from 0.2 to 1
- ramp_rate: float32 [8, 1024], P(None, 'region'), may hold values from 0.1 to 1
- network: float32 [1024, 1024], P('region'), as said below
- pattern: int32 [8, 8], replicated, may hold values from 0 to 1, as said below
- live_hours: int32 [1], replicated, may hold values from 1961 to 2100
- generation: float32 [2240, 8, 1024], P('hour', None, 'region'), may hold values from 0 to 1
- angles: float32 [2240, 1024], P('hour', 'region'), may hold values from -3 to 3
- levels: float32 [2240, 1024], P('hour', 'region'), may hold values from 0 to 2
- net_power: float32 [2240, 1024], P('hour', 'region'), may hold values from -3 to 3
- capacity: float32 [8, 1024], P(None, 'region'), may hold values from 0.5 to 2
- balance_dual: float32 [2240, 1024], P('hour', 'region'), may hold values from -3 to 3
- storage_dual: float32 [2240, 1024], P('hour', 'region'), may hold values from -3 to 3
- limit_dual: float32 [2240, 8, 1024], P('hour', None, 'region'), may hold values from 0 to 1.5
- ramp_dual: float32 [2240, 8, 1024], P('hour', None, 'region'), may hold values from 0 to 0.5
Outputs:
- final_generation: float32 [2240, 8, 1024], P('hour', None, 'region')
- final_angles: float32 [2240, 1024], P('hour', 'region')
- final_levels: float32 [2240, 1024], P('hour', 'region')
- final_power: float32 [2240, 1024], P('hour', 'region')
- final_capacity: float32 [8, 1024], P(None, 'region')
- final_balance: float32 [2240, 1024], P('hour', 'region')
- final_storage: float32 [2240, 1024], P('hour', 'region')
- final_limit: float32 [2240, 8, 1024], P('hour', None, 'region')
- final_ramp: float32 [2240, 8, 1024], P('hour', None, 'region')
Inputs may be any that keep to these rules, and one draw needn't show every extreme that they name: pattern is symmetric with ones on its diagonal. network is symmetric.
All inputs are finite; a program needn't handle non-finite values. No bound on the sum of `tech_mask` on one device may be relied on, other than what follows from the above.
Results may differ from a plain program's by a relative error of at most 0.0003.
Values sent between devices are 32-bit elements; how exact they have to be, the bound alone decides.
No kernel may reach another device: no remote copies, remote signals or barrier semaphores. Data moves between devices by JAX's collectives and lax.ppermute only.
A program may use at most 64 MiB of HBM per device.

v0:
```python
import jax
import jax.numpy as jnp
from jax import lax
from jax.sharding import PartitionSpec as P

BUS = 1024
TECH = 8
BLOCK = 128
ITERS = 2
primal_step = 0.2
capacity_step = 4.0
dual_scale = 0.06


def shifted(block, axis, distance):
    devices = range(lax.axis_size(axis))
    route = [((i - distance) % len(devices), i) for i in devices]
    return lax.ppermute(block, axis, route)


def per_device(
    demand,
    avail_factor,
    tech_mask,
    var_cost,
    inv_cost,
    ramp_rate,
    network,
    pattern,
    live_hours,
    generation,
    angles,
    levels,
    net_power,
    capacity,
    balance_dual,
    storage_dual,
    limit_dual,
    ramp_dual,
):
    hour_rows = demand.shape[0]
    local_bus = demand.shape[1]
    total_hours = hour_rows * lax.axis_size("hour")
    first_hour = lax.axis_index("hour") * hour_rows
    live_rows = (first_hour + jnp.arange(hour_rows, dtype=jnp.int32) < live_hours[0]).astype(
        jnp.float32
    )
    available = (
        avail_factor.astype(jnp.float32)
        * tech_mask.astype(jnp.float32)[None]
        * live_rows[:, None, None]
    )
    live_load = demand * live_rows[:, None]
    blocks_here = local_bus // BLOCK
    pattern_rows = lax.dynamic_slice_in_dim(
        pattern, lax.axis_index("region") * blocks_here, blocks_here, 0
    )
    block_mask = jnp.repeat(jnp.repeat(pattern_rows.astype(jnp.float32), BLOCK, 0), BLOCK, 1)
    matrix = network * block_mask
    entry_count = float(total_hours * (TECH + 3) * BUS)

    def fold_part(segment):
        return lax.dot_general(
            segment,
            matrix,
            (((1,), (1,)), ((), ())),
            precision=lax.Precision.HIGHEST,
            preferred_element_type=jnp.float32,
        )

    for iteration in range(ITERS):
        behind = shifted((ramp_dual[-1:], storage_dual[-1:]), "hour", 1)
        prev_ramp = jnp.concatenate([behind[0], ramp_dual[:-1]], axis=0)
        prev_store = jnp.concatenate([behind[1], storage_dual[:-1]], axis=0)
        gen_new = jnp.maximum(
            0.0,
            generation
            - primal_step
            * (var_cost[None] + balance_dual[:, None, :] + limit_dual + prev_ramp - ramp_dual),
        )
        ang_new = angles + primal_step * fold_part(
            lax.all_gather(balance_dual, "region", axis=1, tiled=True)
        )
        pow_new = net_power - primal_step * (balance_dual + storage_dual)
        lev_new = jnp.maximum(0.0, levels - primal_step * (prev_store - storage_dual))
        square_part = (
            jnp.sum((gen_new - generation) ** 2)
            + jnp.sum((ang_new - angles) ** 2)
            + jnp.sum((pow_new - net_power) ** 2)
            + jnp.sum((lev_new - levels) ** 2)
        )
        invest_part = jnp.sum(available * limit_dual + ramp_rate[None] * ramp_dual, axis=0)
        invest = lax.psum(invest_part, "hour")
        squares = lax.psum(square_part, ("hour", "region"))
        cap_new = jnp.maximum(
            0.0, capacity - capacity_step * (inv_cost - invest / float(total_hours))
        )
        step_size = jnp.sqrt(squares / entry_count + 1e-06)
        dual_step = dual_scale / step_size
        gen_bar = 2.0 * gen_new - generation
        ang_bar = 2.0 * ang_new - angles
        pow_bar = 2.0 * pow_new - net_power
        lev_bar = 2.0 * lev_new - levels
        cap_bar = 2.0 * cap_new - capacity
        forward = shifted((gen_bar[:1], lev_bar[:1]), "hour", -1)
        next_gen = jnp.concatenate([gen_bar[1:], forward[0]], axis=0)
        next_level = jnp.concatenate([lev_bar[1:], forward[1]], axis=0)
        balance_dual = balance_dual + dual_step * (
            jnp.sum(gen_bar, axis=1)
            + pow_bar
            - fold_part(lax.all_gather(ang_bar, "region", axis=1, tiled=True))
            - live_load
        )
        storage_dual = storage_dual + dual_step * (next_level - lev_bar + pow_bar)
        limit_dual = jnp.maximum(
            0.0, limit_dual + dual_step * (gen_bar - available * cap_bar[None])
        )
        ramp_dual = jnp.maximum(
            0.0, ramp_dual + dual_step * (next_gen - gen_bar - ramp_rate[None] * cap_bar[None])
        )
        generation, angles, net_power, levels, capacity = (
            gen_new,
            ang_new,
            pow_new,
            lev_new,
            cap_new,
        )
    return (
        generation,
        angles,
        levels,
        net_power,
        capacity,
        balance_dual,
        storage_dual,
        limit_dual,
        ramp_dual,
    )


def solution(mesh):
    return jax.shard_map(
        per_device,
        mesh=mesh,
        in_specs=(
            P("hour", "region"),
            P("hour", None, "region"),
            P(None, "region"),
            P(None, "region"),
            P(None, "region"),
            P(None, "region"),
            P("region", None),
            P(),
            P(),
            P("hour", None, "region"),
            P("hour", "region"),
            P("hour", "region"),
            P("hour", "region"),
            P(None, "region"),
            P("hour", "region"),
            P("hour", "region"),
            P("hour", None, "region"),
            P("hour", None, "region"),
        ),
        out_specs=(
            P("hour", None, "region"),
            P("hour", "region"),
            P("hour", "region"),
            P("hour", "region"),
            P(None, "region"),
            P("hour", "region"),
            P("hour", "region"),
            P("hour", None, "region"),
            P("hour", None, "region"),
        ),
        check_vma=False,
    )
```

profile of v0, /device:TPU:0, one launch (start us, length us, event | category | flops | bytes accessed | tf_op | source)
XLA Modules:
  0.0 319.3 jit_solution(14245832103954252068)
XLA Ops:
  0.6 0.7 slice.50
  1.4 2.9 collective-permute-start.1
  4.3 0.7 slice.48
  5.0 1.5 collective-permute-start
  7.2 2.4 all_gather.12
  9.6 0.8 dynamic-slice_convert_fusion
  10.5 0.6 broadcast_in_dim.5
  11.2 0.7 bitcast_multiply_fusion
  11.9 0.2 copy-done.28
  12.2 3.7 %multiply_subtract_fusion.7 = (f32[140,512]{1,0:T(8,128)S(1)}, f32[]{:T(128)}, f32[140,512]{1,0:T(8,128)}) fusion(f32[140,512]{1,0:T(8,128)S(1)} %copy-done.28, f32[512,1024]{1,0:T(8,128)S(1)} %bitcast_multiply_fusion, f32[140,1024]{1,0:T(8,128)S(1)} %all_gather.12), kind=kOutput, calls=%fused_computation.61 | convolution fusion | flops 881305600 | bytes 3530756 | tf_op jit(solution)/shard_map/dot_general | solution.py:63
  15.9 2.2 all_gather.13
  18.1 3.0 fusion.39
  21.2 0.6 copy-done.36
  21.9 0.2 copy-done.15
  22.3 3.0 multiply_subtract_fusion.6
  25.3 0.7 multiply_reduce_fusion.5
  26.1 4.1 %collective-permute-start.4 = (f32[1,512]{1,0:T(1,128)S(1)}, f32[1,512]{1,0:T(1,128)S(1)}, u32[]{:S(2)}, u32[]{:S(2)}) collective-permute-start(f32[1,512]{1,0:T(1,128)S(1)} %slice.69), channel_id=1, source_target_pairs={{2,0},{4,2},{6,4},{8,6},{10,8},{12,10},{14,12},{16,14},{18,16},{20... | collective-permute-start | bytes 6152 | tf_op jit(solution)/shard_map/ppermute | solution.py:18
  30.2 6.1 %fusion.36 = (f32[140,512]{1,0:T(8,128)}, f32[140,8,512]{2,1,0:T(8,128)}, f32[140,8,512]{2,1,0:T(8,128)S(1)}, f32[8,512]{1,0:T(8,128)S(1)}) fusion(f32[140,8,512]{2,1,0:T(8,128)} %param.27, f32[140,8,512]{2,1,0:T(8,128)S(1)} %copy-done.5, f32[139,8,512]{2,1,0:T(8,128)S(1)} %slice-done, f32[1,8,512]{2,1,0:T(8,128)S(1)} %collective-permute-done, ...), kind=kLoop, calls=%fused_computation.74 | loop fusion | flops 10246144 | bytes 15548976 | tf_op jit(solution)/shard_map/reduce_sum | solution.py:109
  36.3 1.3 multiply_reduce_fusion.1
  40.2 1.7 slice.68
  41.9 37.6 %psum.28 = f32[]{:T(128)} all-reduce(f32[]{:T(128)S(6)} %add.149), channel_id=1, replica_groups=mesh['hour'=16,'region'=2] {'hour','region'}, use_global_device_ids=true, to_apply=%region_4.0 | all-reduce | flops 1 | bytes 8 | tf_op jit(solution)/shard_map/psum | solution.py:94
  80.3 3.3 %multiply_reduce_fusion.3 = (f32[]{:T(128)}, f32[140,512]{1,0:T(8,128)}, f32[140,512]{1,0:T(8,128)S(1)}, f32[140,512]{1,0:T(8,128)}) fusion(f32[140,512]{1,0:T(8,128)} %get-tuple-element.42, f32[140,512]{1,0:T(8,128)} %param.33, f32[140,512]{1,0:T(8,128)} %param.30, f32[140,512]{1,0:T(8,128)} %copy-done.20, f32[1,512]{1,0:T(1,128)S(1)} %collective-permute-done.4, ...), kind=kLoop, calls=%fused_computation.56 | loop fusion | flops 1361919 | bytes 3441208 | tf_op jit(solution)/shard_map/reduce_sum | solution.py:89
  83.6 0.7 copy-done.10
  84.3 2.3 collective-permute-start.5
  86.6 75.0 %psum.29 = f32[8,512]{1,0:T(8,128)S(1)} all-reduce(f32[8,512]{1,0:T(8,128)S(1)} %get-tuple-element.32), channel_id=1, replica_groups=mesh['hour'=16,'region'=2] {'hour'}, use_global_device_ids=true, to_apply=%region_7.0 | all-reduce | flops 4096 | bytes 32768 | tf_op jit(solution)/shard_map/psum | solution.py:93
  161.5 0.9 slice.65
  162.4 2.6 all_gather.14
  165.0 4.8 %multiply_reduce_fusion.4 = (f32[]{:T(128)}, f32[140,512]{1,0:T(8,128)}, f32[140,512]{1,0:T(8,128)}) fusion(f32[140,512]{1,0:T(8,128)} %get-tuple-element.43, f32[140,1024]{1,0:T(8,128)S(1)} %all_gather.14, f32[512,1024]{1,0:T(8,128)S(1)} %bitcast_multiply_fusion), kind=kOutput, calls=%fused_computation.57 | convolution fusion | flops 881305600 | bytes 3530756 | tf_op jit(solution)/shard_map/dot_general | solution.py:63
  169.9 0.2 slice.64
  170.1 0.7 copy-done.11
  170.9 0.8 multiply_subtract_fusion.2
  171.7 0.9 fusion.7
  172.6 2.1 collective-permute-start.3
  174.7 0.7 multiply_reduce_fusion.2
  175.3 0.2 slice.67
  175.5 4.4 %collective-permute-done.3 = f32[1,8,512]{2,1,0:T(8,128)S(1)} collective-permute-done((f32[1,8,512]{2,1,0:T(8,128)S(1)}, f32[1,8,512]{2,1,0:T(8,128)S(1)}, u32[]{:S(2)}, u32[]{:S(2)}) %collective-permute-start.3) | collective-permute-done | bytes 16416 | tf_op jit(solution)/shard_map/ppermute | solution.py:18
  180.0 4.3 %multiply_reduce_fusion = (f32[]{:T(128)}, f32[140,8,512]{2,1,0:T(8,128)}, f32[140,8,512]{2,1,0:T(8,128)}) fusion(f32[140,8,512]{2,1,0:T(8,128)S(1)} %copy-done.3, f32[140,8,512]{2,1,0:T(8,128)S(1)} %fusion.7, f32[139,8,512]{2,1,0:T(8,128)S(1)} %slice.67, f32[1,8,512]{2,1,0:T(8,128)S(1)} %collective-permute-done.3, f32[140,512]{1,0:T(8,128)S(1)} %copy-done.16, ...), kind=kLoop, calls=%fused_computation.22 | loop fusion | flops 10895359 | bytes 17539640 | tf_op jit(solution)/shard_map/reduce_sum | solution.py:87
  186.8 3.9 %all_gather.15 = f32[140,1024]{1,0:T(8,128)} all-gather(f32[140,512]{1,0:T(8,128)} %get-tuple-element.38), channel_id=1, replica_groups=mesh['hour'=16,'region'=2] {'region'}, dimensions={1}, use_global_device_ids=true | all-gather | bytes 860160 | tf_op jit(solution)/shard_map/all_gather | solution.py:111
  190.7 36.8 %psum.31 = f32[]{:T(128)} all-reduce(f32[]{:T(128)S(6)} %add.169), channel_id=1, replica_groups=mesh['hour'=16,'region'=2] {'hour','region'}, use_global_device_ids=true, to_apply=%region_14.0 | all-reduce | flops 1 | bytes 8 | tf_op jit(solution)/shard_map/psum | solution.py:94
  228.2 2.2 add_reduce_fusion
  230.4 75.8 %psum.30 = f32[8,512]{1,0:T(8,128)S(1)} all-reduce(f32[8,512]{1,0:T(8,128)S(1)} %add_reduce_fusion), channel_id=1, replica_groups=mesh['hour'=16,'region'=2] {'hour'}, use_global_device_ids=true, to_apply=%region_9.0 | all-reduce | flops 4096 | bytes 32768 | tf_op jit(solution)/shard_map/psum | solution.py:93
  306.2 0.6 fusion.31
  306.9 5.3 %add_maximum_fusion = (f32[140,8,512]{2,1,0:T(8,128)}, f32[140,8,512]{2,1,0:T(8,128)S(1)}) fusion(f32[140,8,512]{2,1,0:T(8,128)} %get-tuple-element.22, bf16[140,8,512]{2,1,0:T(8,128)(2,1)S(1)} %copy-done.7, f32[8,512]{1,0:T(8,128)S(1)} %get-tuple-element.10, f32[]{:T(128)S(6)} %div.23, f32[140]{0:T(256)} %copy-done.33, ...), kind=kLoop, calls=%fused_computation.20 | loop fusion | flops 5734400 | bytes 12649012 | tf_op jit(solution)/shard_map/max | solution.py:115
  312.2 2.3 fusion.40
  314.7 0.2 slice.74
  314.9 1.1 collective-permute-done.7
  316.0 2.3 fusion.15
  318.3 1.0 fusion.30
  (90 shorter events, 0.8 us)
Async XLA Ops:
  1.4 20.5 %collective-permute-start.1 = (f32[1,512]{1,0:T(1,128)S(1)}, f32[1,512]{1,0:T(1,128)S(1)}, u32[]{:S(2)}, u32[]{:S(2)}) collective-permute-start(f32[1,512]{1,0:T(1,128)S(1)} %slice.50), channel_id=1, source_target_pairs={{30,0},{0,2},{2,4},{4,6},{6,8},{8,10},{10,12},{12,14},{14,16},{16,... | collective-permute-start | bytes 6152 | tf_op jit(solution)/shard_map/ppermute | solution.py:18
  5.0 25.2 %collective-permute-start = (f32[1,8,512]{2,1,0:T(8,128)S(1)}, f32[1,8,512]{2,1,0:T(8,128)S(1)}, u32[]{:S(2)}, u32[]{:S(2)}) collective-permute-start(f32[1,8,512]{2,1,0:T(8,128)S(1)} %slice.48), channel_id=1, source_target_pairs={{30,0},{0,2},{2,4},{4,6},{6,8},{8,10},{10,12},{12,14},{14,16},{16,... | collective-permute-start | bytes 49160 | tf_op jit(solution)/shard_map/ppermute | solution.py:18
  9.6 1.6 copy-start.23
  11.2 1.0 copy-start.28
  12.2 152.8 %copy-start = (f32[512,1024]{1,0:T(8,128)}, f32[512,1024]{1,0:T(8,128)S(1)}, u32[]{:S(2)}) copy-start(f32[512,1024]{1,0:T(8,128)S(1)} %bitcast_multiply_fusion) | copy-start | bytes 6291460
  21.1 0.7 copy-start.36
  21.1 59.1 %copy-start.33 = (f32[140]{0:T(256)}, f32[140]{0:T(256)S(1)}, u32[]{:S(2)}) copy-start(f32[140]{0:T(256)S(1)} %compare_convert_fusion) | copy-start | bytes 1684
  21.1 1.0 copy-start.15
  21.2 1.0 copy-start.18
  21.2 1.1 copy-start.24
  21.2 9.0 %copy-start.5 = (f32[140,8,512]{2,1,0:T(8,128)S(1)}, f32[140,8,512]{2,1,0:T(8,128)}, u32[]{:S(2)}) copy-start(f32[140,8,512]{2,1,0:T(8,128)} %param.35) | copy-start | bytes 6881284
  21.2 9.0 %copy-start.7 = (bf16[140,8,512]{2,1,0:T(8,128)(2,1)S(1)}, bf16[140,8,512]{2,1,0:T(8,128)(2,1)}, u32[]{:S(2)}) copy-start(bf16[140,8,512]{2,1,0:T(8,128)(2,1)} %param.19) | copy-start | bytes 3440644
  21.9 8.4 %slice-start = ((f32[140,8,512]{2,1,0:T(8,128)}), f32[139,8,512]{2,1,0:T(8,128)S(1)}, s32[]{:S(2)}) async-start(f32[140,8,512]{2,1,0:T(8,128)} %param.35), calls=%async_computation | async-start | bytes 4554752 | tf_op jit(solution)/shard_map/slice | solution.py:73
  21.9 8.4 %copy-start.29 = (f32[8,512]{1,0:T(8,128)S(1)}, f32[8,512]{1,0:T(8,128)}, u32[]{:S(2)}) copy-start(f32[8,512]{1,0:T(8,128)} %param.23) | copy-start | bytes 49156
  21.9 8.4 %copy-start.32 = (f32[8,512]{1,0:T(8,128)S(1)}, f32[8,512]{1,0:T(8,128)}, u32[]{:S(2)}) copy-start(f32[8,512]{1,0:T(8,128)} %param.21) | copy-start | bytes 49156
  25.3 0.7 copy-start.20
  25.3 4.8 %copy-start.13 = (f32[140,512]{1,0:T(8,128)}, f32[140,512]{1,0:T(8,128)S(1)}, u32[]{:S(2)}) copy-start(f32[140,512]{1,0:T(8,128)S(1)} %get-tuple-element.24) | copy-start | bytes 860164
  26.1 10.3 %copy-start.8 = (f32[140,8,512]{2,1,0:T(8,128)S(1)}, f32[140,8,512]{2,1,0:T(8,128)}, u32[]{:S(2)}) copy-start(f32[140,8,512]{2,1,0:T(8,128)} %param.27) | copy-start | bytes 6881284
  26.1 54.2 %collective-permute-start.4 = (f32[1,512]{1,0:T(1,128)S(1)}, f32[1,512]{1,0:T(1,128)S(1)}, u32[]{:S(2)}, u32[]{:S(2)}) collective-permute-start(f32[1,512]{1,0:T(1,128)S(1)} %slice.69), channel_id=1, source_target_pairs={{2,0},{4,2},{6,4},{8,6},{10,8},{12,10},{14,12},{16,14},{18,16},{20... | collective-permute-start | bytes 6152 | tf_op jit(solution)/shard_map/ppermute | solution.py:18
  36.3 1.4 copy-start.2
  83.6 0.7 copy-start.10
  83.6 86.2 %copy-start.30 = (f32[8,512]{1,0:T(8,128)S(1)}, f32[8,512]{1,0:T(8,128)}, u32[]{:S(2)}) copy-start(f32[8,512]{1,0:T(8,128)} %param.31) | copy-start | bytes 49156
  83.6 86.2 %copy-start.31 = (f32[8,512]{1,0:T(8,128)S(1)}, f32[8,512]{1,0:T(8,128)}, u32[]{:S(2)}) copy-start(f32[8,512]{1,0:T(8,128)} %param.22) | copy-start | bytes 49156
  84.3 85.8 %collective-permute-start.5 = (f32[1,512]{1,0:T(1,128)S(1)}, f32[1,512]{1,0:T(1,128)S(1)}, u32[]{:S(2)}, u32[]{:S(2)}) collective-permute-start(f32[1,512]{1,0:T(1,128)S(1)} %slice.70), channel_id=1, source_target_pairs={{30,0},{0,2},{2,4},{4,6},{6,8},{8,10},{10,12},{12,14},{14,16},{16,... | collective-permute-start | bytes 6152 | tf_op jit(solution)/shard_map/ppermute | solution.py:18
  161.5 8.3 %copy-start.4 = (f32[140,8,512]{2,1,0:T(8,128)S(1)}, f32[140,8,512]{2,1,0:T(8,128)}, u32[]{:S(2)}) copy-start(f32[140,8,512]{2,1,0:T(8,128)} %get-tuple-element.26) | copy-start | bytes 6881284
  162.4 9.3 %collective-permute-start.2 = (f32[1,8,512]{2,1,0:T(8,128)S(1)}, f32[1,8,512]{2,1,0:T(8,128)S(1)}, u32[]{:S(2)}, u32[]{:S(2)}) collective-permute-start(f32[1,8,512]{2,1,0:T(8,128)S(1)} %slice.65), channel_id=1, source_target_pairs={{2,0},{4,2},{6,4},{8,6},{10,8},{12,10},{14,12},{16,14},{18,16},{20... | collective-permute-start | bytes 49160 | tf_op jit(solution)/shard_map/ppermute | solution.py:18
  169.9 1.0 copy-start.11
  169.9 1.0 copy-start.14
  169.9 1.9 copy-start.6
  171.7 3.0 copy-start.27
  172.6 7.4 %collective-permute-start.3 = (f32[1,8,512]{2,1,0:T(8,128)S(1)}, f32[1,8,512]{2,1,0:T(8,128)S(1)}, u32[]{:S(2)}, u32[]{:S(2)}) collective-permute-start(f32[1,8,512]{2,1,0:T(8,128)S(1)} %slice.66), channel_id=1, source_target_pairs={{30,0},{0,2},{2,4},{4,6},{6,8},{8,10},{10,12},{12,14},{14,16},{16,... | collective-permute-start | bytes 49160 | tf_op jit(solution)/shard_map/ppermute | solution.py:18
  174.7 5.3 %copy-start.9 = (f32[140,8,512]{2,1,0:T(8,128)S(1)}, f32[140,8,512]{2,1,0:T(8,128)}, u32[]{:S(2)}) copy-start(f32[140,8,512]{2,1,0:T(8,128)} %param.34) | copy-start | bytes 6881284
  175.3 4.7 %copy-start.3 = (f32[140,8,512]{2,1,0:T(8,128)S(1)}, f32[140,8,512]{2,1,0:T(8,128)}, u32[]{:S(2)}) copy-start(f32[140,8,512]{2,1,0:T(8,128)} %copy-done.2) | copy-start | bytes 6881284
  175.3 4.7 %copy-start.16 = (f32[140,512]{1,0:T(8,128)S(1)}, f32[140,512]{1,0:T(8,128)}, u32[]{:S(2)}) copy-start(f32[140,512]{1,0:T(8,128)} %get-tuple-element.19) | copy-start | bytes 860164
  175.3 4.7 %copy-start.34 = (f32[140]{0:T(256)S(1)}, f32[140]{0:T(256)}, u32[]{:S(2)}) copy-start(f32[140]{0:T(256)} %copy-done.33) | copy-start | bytes 1684
  306.9 5.4 %copy-start.1 = (f32[512,1024]{1,0:T(8,128)S(1)}, f32[512,1024]{1,0:T(8,128)}, u32[]{:S(2)}) copy-start(f32[512,1024]{1,0:T(8,128)} %copy-done) | copy-start | bytes 6291460
  306.9 5.4 %copy-start.22 = (f32[140,1024]{1,0:T(8,128)S(1)}, f32[140,1024]{1,0:T(8,128)}, u32[]{:S(2)}) copy-start(f32[140,1024]{1,0:T(8,128)} %all_gather.15) | copy-start | bytes 1720324
  312.2 2.4 copy-start.19
  312.2 3.7 %collective-permute-start.7 = (f32[1,8,512]{2,1,0:T(8,128)S(1)}, f32[1,8,512]{2,1,0:T(8,128)S(1)}, u32[]{:S(2)}, u32[]{:S(2)}) collective-permute-start(f32[1,8,512]{2,1,0:T(8,128)S(1)} %slice.75), channel_id=1, source_target_pairs={{2,0},{4,2},{6,4},{8,6},{10,8},{12,10},{14,12},{16,14},{18,16},{20... | collective-permute-start | bytes 49160 | tf_op jit(solution)/shard_map/ppermute | solution.py:18
  314.6 3.6 %collective-permute-start.6 = (f32[1,512]{1,0:T(1,128)S(1)}, f32[1,512]{1,0:T(1,128)S(1)}, u32[]{:S(2)}, u32[]{:S(2)}) collective-permute-start(f32[1,512]{1,0:T(1,128)S(1)} %slice.73), channel_id=1, source_target_pairs={{2,0},{4,2},{6,4},{8,6},{10,8},{12,10},{14,12},{16,14},{18,16},{20... | collective-permute-start | bytes 6152 | tf_op jit(solution)/shard_map/ppermute | solution.py:18
  315.9 2.3 copy-start.12
  315.9 2.3 copy-start.17
  315.9 2.3 copy-start.21
  316.0 2.3 copy-start.25
  316.0 2.3 copy-start.26
  316.0 2.3 copy-start.35
where the time goes:
time: 320 us; the launch traced here: 319 us
  blocking collectives  236 us (74%)
  other arithmetic  34 us (11%)
  matrix products  13.8 us (4%)
  starting transfers between devices  13 us (4%)
  local copies, waits for them, and re-layouts  8.49 us (3%)
  between operations  8.08 us (3%)
  waiting for transfers between devices  5.53 us (2%)
    psum x2, blocking collectives, per_device(): invest = lax.psum(invest_part, 'hour')  151 us
    psum x2, blocking collectives, per_device(): squares = lax.psum(square_part, ('hour', 'region'))  74.5 us
    dot_general x4, matrix products, fold_part(): lax.dot_general(segment, matrix, (((1,), (1,)), ((), ())), precision=lax....  13.8 us
    ppermute x8, starting transfers between devices, shifted(): return lax.ppermute(block, axis, route)  13 us
  transfers between devices with their start and end apart: 8, of which 2 were waited for; matrix products, arithmetic and copies ran while one was open for 11% of the time, Pallas kernels for 0%

commit v1 on v0

--- a/solution.py
+++ b/solution.py
@@ -91,7 +91,7 @@
         )
         invest_part = jnp.sum(available * limit_dual + ramp_rate[None] * ramp_dual, axis=0)
         invest = lax.psum(invest_part, "hour")
-        squares = lax.psum(square_part, ("hour", "region"))
+        squares = lax.psum(lax.psum(square_part, "region"), "hour")
         cap_new = jnp.maximum(
             0.0, capacity - capacity_step * (inv_cost - invest / float(total_hours))
         )

time: 320 us -> 248 us (0.78)
  blocking collectives: 236 us -> 161 us
    psum x2, blocking collectives: 74.5 us -> 5.94 us  [per_device(): squares = lax.psum(lax.psum(square_part, 'region'), 'hour')]
    psum x2, blocking collectives: 151 us -> 144 us  [per_device(): invest = lax.psum(invest_part, 'hour')]
where the time goes in v1:
time: 248 us; the launch traced here: 247 us
  blocking collectives  161 us (65%)
  other arithmetic  35.8 us (14%)
  starting transfers between devices  14.4 us (6%)
  matrix products  13.9 us (6%)
  between operations  8.3 us (3%)
  waiting for transfers between devices  7.44 us (3%)
  local copies, waits for them, and re-layouts  6.15 us (2%)
    psum x2, blocking collectives, per_device(): invest = lax.psum(invest_part, 'hour')  144 us
    ppermute x8, starting transfers between devices, shifted(): return lax.ppermute(block, axis, route)  14.4 us
    dot_general x4, matrix products, fold_part(): lax.dot_general(segment, matrix, (((1,), (1,)), ((), ())), precision=lax....  13.9 us
    ppermute x8, waiting for transfers between devices, shifted(): return lax.ppermute(block, axis, route)  7.44 us
    all_gather x2, blocking collectives, per_device(): lax.all_gather(ang_bar, 'region', axis=1, tiled=True)  6.1 us
    psum x2, blocking collectives, per_device(): squares = lax.psum(lax.psum(square_part, 'region'), 'hour')  5.94 us
    reduce_sum x1, other arithmetic, per_device(): jnp.sum(gen_bar, axis=1) + pow_bar  5.8 us
    reduce_sum x2, other arithmetic, per_device(): jnp.sum((gen_new - generation) ** 2) + jnp.sum((ang_new - angles) ** 2)  5.61 us
  transfers between devices with their start and end apart: 8, of which 2 were waited for; matrix products, arithmetic and copies ran while one was open for 11% of the time, Pallas kernels for 0%

profile of v1, /device:TPU:0, one launch (start us, length us, event | category | flops | bytes accessed | tf_op | source)
XLA Modules:
  0.0 247.3 jit_solution(16707573921216332136)
XLA Ops:
  0.6 0.7 slice.50
  1.4 2.9 %collective-permute-start.1 = (f32[1,512]{1,0:T(1,128)S(1)}, f32[1,512]{1,0:T(1,128)S(1)}, u32[]{:S(2)}, u32[]{:S(2)}) collective-permute-start(f32[1,512]{1,0:T(1,128)S(1)} %slice.50), channel_id=1, source_target_pairs={{30,0},{0,2},{2,4},{4,6},{6,8},{8,10},{10,12},{12,14},{14,16},{16,... | collective-permute-start | bytes 6152 | tf_op jit(solution)/shard_map/ppermute | solution.py:18
  4.3 0.7 slice.48
  5.0 1.5 collective-permute-start
  7.2 2.4 all_gather.12
  9.6 0.8 dynamic-slice_convert_fusion
  10.5 0.6 broadcast_in_dim.5
  11.1 0.1 copy-done.20
  11.2 0.7 bitcast_multiply_fusion
  11.9 0.2 copy-done.24
  12.2 3.7 %multiply_subtract_fusion.7 = (f32[140,512]{1,0:T(8,128)S(1)}, f32[]{:T(128)}, f32[140,512]{1,0:T(8,128)}) fusion(f32[140,512]{1,0:T(8,128)S(1)} %copy-done.24, f32[512,1024]{1,0:T(8,128)S(1)} %bitcast_multiply_fusion, f32[140,1024]{1,0:T(8,128)S(1)} %all_gather.12), kind=kOutput, calls=%fused_computation.61 | convolution fusion | flops 881305600 | bytes 3530756 | tf_op jit(solution)/shard_map/dot_general | solution.py:63
  15.9 2.2 all_gather.13
  18.1 3.0 %fusion.39 = f32[140,512]{1,0:T(8,128)} fusion(f32[140,1024]{1,0:T(8,128)S(1)} %all_gather.13, f32[512,1024]{1,0:T(8,128)S(1)} %bitcast_multiply_fusion), kind=kOutput, calls=%fused_computation.76 | convolution fusion | flops 880803840 | bytes 2957312 | tf_op jit(solution)/shard_map/dot_general | solution.py:63
  21.2 0.7 copy-done.32
  21.9 3.2 %multiply_subtract_fusion.6 = (f32[140,512]{1,0:T(8,128)S(1)}, f32[140,512]{1,0:T(8,128)S(1)}, f32[]{:T(128)}, f32[140,512]{1,0:T(8,128)}) fusion(f32[140,512]{1,0:T(8,128)} %param.29, f32[140,512]{1,0:T(8,128)} %param.33, f32[139,512]{1,0:T(8,128)} %bitcast.22, f32[1,512]{1,0:T(1,128)S(1)} %collective-permute-done.1, f32[140,512]{1,0:T(8,128)} %param.30, ...), kind=kLoop, calls=%fused_computation.59 | loop fusion | flops 931839 | bytes 2293764 | tf_op jit(solution)/shard_map/sub | solution.py:103
  25.2 1.9 multiply_reduce_fusion.5
  27.1 0.7 slice.68
  27.9 5.8 %fusion.36 = (f32[140,512]{1,0:T(8,128)}, f32[140,8,512]{2,1,0:T(8,128)}, f32[140,8,512]{2,1,0:T(8,128)S(1)}, f32[8,512]{1,0:T(8,128)S(1)}) fusion(f32[140,8,512]{2,1,0:T(8,128)S(1)} %copy-done.8, f32[140,8,512]{2,1,0:T(8,128)S(1)} %copy-done.5, f32[139,8,512]{2,1,0:T(8,128)S(1)} %slice-done, f32[1,8,512]{2,1,0:T(8,128)S(1)} %collective-permute-done, ...), kind=kLoop, calls=%fused_computation.74 | loop fusion | flops 10246144 | bytes 15548976 | tf_op jit(solution)/shard_map/reduce_sum | solution.py:109
  33.7 1.3 multiply_reduce_fusion.1
  35.0 0.1 copy-done.2
  37.7 4.2 %collective-permute-start.4 = (f32[1,512]{1,0:T(1,128)S(1)}, f32[1,512]{1,0:T(1,128)S(1)}, u32[]{:S(2)}, u32[]{:S(2)}) collective-permute-start(f32[1,512]{1,0:T(1,128)S(1)} %slice.69), channel_id=1, source_target_pairs={{2,0},{4,2},{6,4},{8,6},{10,8},{12,10},{14,12},{16,14},{18,16},{20... | collective-permute-start | bytes 6152 | tf_op jit(solution)/shard_map/ppermute | solution.py:18
  41.9 3.0 %psum.42 = f32[]{:T(128)} all-reduce(f32[]{:T(128)S(6)} %add.153), channel_id=1, replica_groups=mesh['hour'=16,'region'=2] {'region'}, use_global_device_ids=true, to_apply=%region_4.0 | all-reduce | flops 1 | bytes 8 | tf_op jit(solution)/shard_map/psum | solution.py:94
  44.8 72.0 %all-reduce.1 = (f32[8,512]{1,0:T(8,128)S(1)}, f32[]{:T(128)}) all-reduce(f32[8,512]{1,0:T(8,128)S(1)} %get-tuple-element.36, f32[]{:T(128)} %psum.42), channel_id=1, replica_groups=mesh['hour'=16,'region'=2] {'hour'}, use_global_device_ids=true, to_apply=%region_8.0 | all-reduce | flops 4097 | bytes 32776 | tf_op jit(solution)/shard_map/psum | solution.py:93
  116.8 0.7 slice.65
  118.3 3.2 %multiply_reduce_fusion.3 = (f32[]{:T(128)}, f32[140,512]{1,0:T(8,128)}, f32[140,512]{1,0:T(8,128)S(1)}, f32[140,512]{1,0:T(8,128)S(1)}) fusion(f32[140,512]{1,0:T(8,128)} %get-tuple-element.46, f32[140,512]{1,0:T(8,128)} %param.33, f32[140,512]{1,0:T(8,128)} %param.30, f32[140,512]{1,0:T(8,128)} %copy-done.17, f32[1,512]{1,0:T(1,128)S(1)} %collective-permute-done.4, ...), kind=kLoop, calls=%fused_computation.56 | loop fusion | flops 1361919 | bytes 3441208 | tf_op jit(solution)/shard_map/reduce_sum | solution.py:89
  121.5 0.1 collective-permute-start.5
  121.5 5.6 %collective-permute-start.2 = (f32[1,8,512]{2,1,0:T(8,128)S(1)}, f32[1,8,512]{2,1,0:T(8,128)S(1)}, u32[]{:S(2)}, u32[]{:S(2)}) collective-permute-start(f32[1,8,512]{2,1,0:T(8,128)S(1)} %slice.65), channel_id=1, source_target_pairs={{2,0},{4,2},{6,4},{8,6},{10,8},{12,10},{14,12},{16,14},{18,16},{20... | collective-permute-start | bytes 49160 | tf_op jit(solution)/shard_map/ppermute | solution.py:18
  127.2 2.4 all_gather.14
  129.6 4.8 %multiply_subtract_fusion.3 = (f32[140,512]{1,0:T(8,128)}, f32[]{:T(128)}, f32[140,512]{1,0:T(8,128)}) fusion(f32[140,512]{1,0:T(8,128)} %get-tuple-element.47, f32[140,1024]{1,0:T(8,128)S(1)} %all_gather.14, f32[512,1024]{1,0:T(8,128)S(1)} %bitcast_multiply_fusion), kind=kOutput, calls=%fused_computation.53 | convolution fusion | flops 881305600 | bytes 3530756 | tf_op jit(solution)/shard_map/dot_general | solution.py:63
  134.4 0.2 slice.64
  134.6 0.7 copy-done.13
  135.3 0.8 multiply_subtract_fusion.2
  136.2 0.9 fusion.7
  137.1 0.7 multiply_reduce_fusion.2
  137.9 0.2 slice.67
  138.1 6.4 %collective-permute-done.3 = f32[1,8,512]{2,1,0:T(8,128)S(1)} collective-permute-done((f32[1,8,512]{2,1,0:T(8,128)S(1)}, f32[1,8,512]{2,1,0:T(8,128)S(1)}, u32[]{:S(2)}, u32[]{:S(2)}) %collective-permute-start.3) | collective-permute-done | bytes 16416 | tf_op jit(solution)/shard_map/ppermute | solution.py:18
  144.5 4.3 %multiply_reduce_fusion = (f32[]{:T(128)}, f32[140,8,512]{2,1,0:T(8,128)}, f32[140,8,512]{2,1,0:T(8,128)}) fusion(f32[140,8,512]{2,1,0:T(8,128)S(1)} %copy-done.3, f32[140,8,512]{2,1,0:T(8,128)S(1)} %fusion.7, f32[139,8,512]{2,1,0:T(8,128)S(1)} %slice.67, f32[1,8,512]{2,1,0:T(8,128)S(1)} %collective-permute-done.3, f32[140,512]{1,0:T(8,128)S(1)} %get-tuple-element.23, ...), kind=kLoop, calls=%fused_computation.22 | loop fusion | flops 10895359 | bytes 17539640 | tf_op jit(solution)/shard_map/reduce_sum | solution.py:87
  151.4 3.9 %all_gather.15 = f32[140,1024]{1,0:T(8,128)} all-gather(f32[140,512]{1,0:T(8,128)} %get-tuple-element.41), channel_id=1, replica_groups=mesh['hour'=16,'region'=2] {'region'}, dimensions={1}, use_global_device_ids=true | all-gather | bytes 860160 | tf_op jit(solution)/shard_map/all_gather | solution.py:111
  155.3 3.0 %psum.46 = f32[]{:T(128)} all-reduce(f32[]{:T(128)S(6)} %add.173), channel_id=1, replica_groups=mesh['hour'=16,'region'=2] {'region'}, use_global_device_ids=true, to_apply=%region_15.0 | all-reduce | flops 1 | bytes 8 | tf_op jit(solution)/shard_map/psum | solution.py:94
  158.3 2.2 add_reduce_fusion
  160.5 72.4 %all-reduce = (f32[8,512]{1,0:T(8,128)}, f32[]{:T(128)}) all-reduce(f32[8,512]{1,0:T(8,128)S(1)} %add_reduce_fusion, f32[]{:T(128)} %psum.46), channel_id=1, replica_groups=mesh['hour'=16,'region'=2] {'hour'}, use_global_device_ids=true, to_apply=%region_10.0 | all-reduce | flops 4097 | bytes 32776 | tf_op jit(solution)/shard_map/psum | solution.py:93
  233.6 1.3 fusion.31
  234.9 5.3 %add_maximum_fusion = (f32[140,8,512]{2,1,0:T(8,128)}, f32[140,8,512]{2,1,0:T(8,128)S(1)}) fusion(f32[140,8,512]{2,1,0:T(8,128)} %get-tuple-element.26, bf16[140,8,512]{2,1,0:T(8,128)(2,1)S(1)} %copy-done.7, f32[8,512]{1,0:T(8,128)S(1)} %get-tuple-element.14, f32[]{:T(128)S(6)} %div.23, f32[140]{0:T(256)S(1)} %copy-done.31, ...), kind=kLoop, calls=%fused_computation.20 | loop fusion | flops 5734400 | bytes 12649012 | tf_op jit(solution)/shard_map/max | solution.py:115
  240.3 2.3 fusion.40
  242.7 0.2 slice.74
  242.9 1.1 collective-permute-done.7
  244.0 2.3 fusion.15
  246.3 1.0 fusion.30
  (82 shorter events, 0.4 us)
Async XLA Ops:
  1.4 20.6 %collective-permute-start.1 = (f32[1,512]{1,0:T(1,128)S(1)}, f32[1,512]{1,0:T(1,128)S(1)}, u32[]{:S(2)}, u32[]{:S(2)}) collective-permute-start(f32[1,512]{1,0:T(1,128)S(1)} %slice.50), channel_id=1, source_target_pairs={{30,0},{0,2},{2,4},{4,6},{6,8},{8,10},{10,12},{12,14},{14,16},{16,... | collective-permute-start | bytes 6152 | tf_op jit(solution)/shard_map/ppermute | solution.py:18
  5.0 22.8 %collective-permute-start = (f32[1,8,512]{2,1,0:T(8,128)S(1)}, f32[1,8,512]{2,1,0:T(8,128)S(1)}, u32[]{:S(2)}, u32[]{:S(2)}) collective-permute-start(f32[1,8,512]{2,1,0:T(8,128)S(1)} %slice.48), channel_id=1, source_target_pairs={{30,0},{0,2},{2,4},{4,6},{6,8},{8,10},{10,12},{12,14},{14,16},{16,... | collective-permute-start | bytes 49160 | tf_op jit(solution)/shard_map/ppermute | solution.py:18
  9.6 1.6 copy-start.20
  11.2 1.0 copy-start.24
  12.2 117.4 %copy-start = (f32[512,1024]{1,0:T(8,128)}, f32[512,1024]{1,0:T(8,128)S(1)}, u32[]{:S(2)}) copy-start(f32[512,1024]{1,0:T(8,128)S(1)} %bitcast_multiply_fusion) | copy-start | bytes 6291460
  21.2 0.7 copy-start.32
  21.2 97.1 %copy-start.29 = (f32[140]{0:T(256)}, f32[140]{0:T(256)S(1)}, u32[]{:S(2)}) copy-start(f32[140]{0:T(256)S(1)} %compare_convert_fusion) | copy-start | bytes 1684
  21.2 6.7 %copy-start.5 = (f32[140,8,512]{2,1,0:T(8,128)S(1)}, f32[140,8,512]{2,1,0:T(8,128)}, u32[]{:S(2)}) copy-start(f32[140,8,512]{2,1,0:T(8,128)} %param.35) | copy-start | bytes 6881284
  21.2 6.7 %copy-start.8 = (f32[140,8,512]{2,1,0:T(8,128)S(1)}, f32[140,8,512]{2,1,0:T(8,128)}, u32[]{:S(2)}) copy-start(f32[140,8,512]{2,1,0:T(8,128)} %param.27) | copy-start | bytes 6881284
  21.9 6.0 %slice-start = ((f32[140,8,512]{2,1,0:T(8,128)}), f32[139,8,512]{2,1,0:T(8,128)S(1)}, s32[]{:S(2)}) async-start(f32[140,8,512]{2,1,0:T(8,128)} %param.35), calls=%async_computation | async-start | bytes 4554752 | tf_op jit(solution)/shard_map/slice | solution.py:73
  21.9 6.0 %copy-start.7 = (bf16[140,8,512]{2,1,0:T(8,128)(2,1)S(1)}, bf16[140,8,512]{2,1,0:T(8,128)(2,1)}, u32[]{:S(2)}) copy-start(bf16[140,8,512]{2,1,0:T(8,128)(2,1)} %param.19) | copy-start | bytes 3440644
  21.9 6.0 %copy-start.25 = (f32[8,512]{1,0:T(8,128)S(1)}, f32[8,512]{1,0:T(8,128)}, u32[]{:S(2)}) copy-start(f32[8,512]{1,0:T(8,128)} %param.23) | copy-start | bytes 49156
  21.9 6.0 %copy-start.28 = (f32[8,512]{1,0:T(8,128)S(1)}, f32[8,512]{1,0:T(8,128)}, u32[]{:S(2)}) copy-start(f32[8,512]{1,0:T(8,128)} %param.21) | copy-start | bytes 49156
  25.2 2.6 %copy-start.12 = (f32[140,512]{1,0:T(8,128)}, f32[140,512]{1,0:T(8,128)S(1)}, u32[]{:S(2)}) copy-start(f32[140,512]{1,0:T(8,128)S(1)} %get-tuple-element.28) | copy-start | bytes 860164
  25.2 2.6 %copy-start.17 = (f32[140,512]{1,0:T(8,128)}, f32[140,512]{1,0:T(8,128)S(1)}, u32[]{:S(2)}) copy-start(f32[140,512]{1,0:T(8,128)S(1)} %get-tuple-element.27) | copy-start | bytes 860164
  33.7 1.4 copy-start.2
  37.7 80.5 %collective-permute-start.4 = (f32[1,512]{1,0:T(1,128)S(1)}, f32[1,512]{1,0:T(1,128)S(1)}, u32[]{:S(2)}, u32[]{:S(2)}) collective-permute-start(f32[1,512]{1,0:T(1,128)S(1)} %slice.69), channel_id=1, source_target_pairs={{2,0},{4,2},{6,4},{8,6},{10,8},{12,10},{14,12},{16,14},{18,16},{20... | collective-permute-start | bytes 6152 | tf_op jit(solution)/shard_map/ppermute | solution.py:18
  121.5 13.2 %copy-start.10 = (f32[140,512]{1,0:T(8,128)}, f32[140,512]{1,0:T(8,128)S(1)}, u32[]{:S(2)}) copy-start(f32[140,512]{1,0:T(8,128)S(1)} %get-tuple-element.22) | copy-start | bytes 860164
  121.5 23.0 %copy-start.14 = (f32[140,512]{1,0:T(8,128)}, f32[140,512]{1,0:T(8,128)S(1)}, u32[]{:S(2)}) copy-start(f32[140,512]{1,0:T(8,128)S(1)} %get-tuple-element.23) | copy-start | bytes 860164
  121.5 12.9 %copy-start.26 = (f32[8,512]{1,0:T(8,128)S(1)}, f32[8,512]{1,0:T(8,128)}, u32[]{:S(2)}) copy-start(f32[8,512]{1,0:T(8,128)} %param.31) | copy-start | bytes 49156
  121.5 12.9 %copy-start.27 = (f32[8,512]{1,0:T(8,128)S(1)}, f32[8,512]{1,0:T(8,128)}, u32[]{:S(2)}) copy-start(f32[8,512]{1,0:T(8,128)} %param.22) | copy-start | bytes 49156
  121.5 12.9 %copy-start.4 = (f32[140,8,512]{2,1,0:T(8,128)S(1)}, f32[140,8,512]{2,1,0:T(8,128)}, u32[]{:S(2)}) copy-start(f32[140,8,512]{2,1,0:T(8,128)} %get-tuple-element.30) | copy-start | bytes 6881284
  121.5 13.1 %collective-permute-start.5 = (f32[1,512]{1,0:T(1,128)S(1)}, f32[1,512]{1,0:T(1,128)S(1)}, u32[]{:S(2)}, u32[]{:S(2)}) collective-permute-start(f32[1,512]{1,0:T(1,128)S(1)} %slice.70), channel_id=1, source_target_pairs={{30,0},{0,2},{2,4},{4,6},{6,8},{8,10},{10,12},{12,14},{14,16},{16,... | collective-permute-start | bytes 6152 | tf_op jit(solution)/shard_map/ppermute | solution.py:18
  121.5 14.6 %collective-permute-start.2 = (f32[1,8,512]{2,1,0:T(8,128)S(1)}, f32[1,8,512]{2,1,0:T(8,128)S(1)}, u32[]{:S(2)}, u32[]{:S(2)}) collective-permute-start(f32[1,8,512]{2,1,0:T(8,128)S(1)} %slice.65), channel_id=1, source_target_pairs={{2,0},{4,2},{6,4},{8,6},{10,8},{12,10},{14,12},{16,14},{18,16},{20... | collective-permute-start | bytes 49160 | tf_op jit(solution)/shard_map/ppermute | solution.py:18
  134.4 1.0 copy-start.13
  134.4 1.8 copy-start.6
  136.2 1.0 copy-start.23
  137.0 7.4 %collective-permute-start.3 = (f32[1,8,512]{2,1,0:T(8,128)S(1)}, f32[1,8,512]{2,1,0:T(8,128)S(1)}, u32[]{:S(2)}, u32[]{:S(2)}) collective-permute-start(f32[1,8,512]{2,1,0:T(8,128)S(1)} %slice.66), channel_id=1, source_target_pairs={{30,0},{0,2},{2,4},{4,6},{6,8},{8,10},{10,12},{12,14},{14,16},{16,... | collective-permute-start | bytes 49160 | tf_op jit(solution)/shard_map/ppermute | solution.py:18
  137.1 7.3 %copy-start.9 = (f32[140,8,512]{2,1,0:T(8,128)S(1)}, f32[140,8,512]{2,1,0:T(8,128)}, u32[]{:S(2)}) copy-start(f32[140,8,512]{2,1,0:T(8,128)} %param.34) | copy-start | bytes 6881284
  137.9 6.6 %copy-start.3 = (f32[140,8,512]{2,1,0:T(8,128)S(1)}, f32[140,8,512]{2,1,0:T(8,128)}, u32[]{:S(2)}) copy-start(f32[140,8,512]{2,1,0:T(8,128)} %copy-done.2) | copy-start | bytes 6881284
  137.9 6.6 %copy-start.30 = (f32[140]{0:T(256)S(1)}, f32[140]{0:T(256)}, u32[]{:S(2)}) copy-start(f32[140]{0:T(256)} %copy-done.29) | copy-start | bytes 1684
  158.3 76.6 %copy-start.31 = (f32[140]{0:T(256)S(1)}, f32[140]{0:T(256)}, u32[]{:S(2)}) copy-start(f32[140]{0:T(256)} %copy-done.29) | copy-start | bytes 1684
  234.9 5.4 %copy-start.1 = (f32[512,1024]{1,0:T(8,128)S(1)}, f32[512,1024]{1,0:T(8,128)}, u32[]{:S(2)}) copy-start(f32[512,1024]{1,0:T(8,128)} %copy-done) | copy-start | bytes 6291460
  234.9 5.4 %copy-start.19 = (f32[140,1024]{1,0:T(8,128)S(1)}, f32[140,1024]{1,0:T(8,128)}, u32[]{:S(2)}) copy-start(f32[140,1024]{1,0:T(8,128)} %all_gather.15) | copy-start | bytes 1720324
  240.2 2.4 copy-start.16
  240.2 3.7 %collective-permute-start.7 = (f32[1,8,512]{2,1,0:T(8,128)S(1)}, f32[1,8,512]{2,1,0:T(8,128)S(1)}, u32[]{:S(2)}, u32[]{:S(2)}) collective-permute-start(f32[1,8,512]{2,1,0:T(8,128)S(1)} %slice.75), channel_id=1, source_target_pairs={{2,0},{4,2},{6,4},{8,6},{10,8},{12,10},{14,12},{16,14},{18,16},{20... | collective-permute-start | bytes 49160 | tf_op jit(solution)/shard_map/ppermute | solution.py:18
  242.7 3.6 %collective-permute-start.6 = (f32[1,512]{1,0:T(1,128)S(1)}, f32[1,512]{1,0:T(1,128)S(1)}, u32[]{:S(2)}, u32[]{:S(2)}) collective-permute-start(f32[1,512]{1,0:T(1,128)S(1)} %slice.73), channel_id=1, source_target_pairs={{2,0},{4,2},{6,4},{8,6},{10,8},{12,10},{14,12},{16,14},{18,16},{20... | collective-permute-start | bytes 6152 | tf_op jit(solution)/shard_map/ppermute | solution.py:18
  244.0 2.3 copy-start.11
  244.0 2.3 copy-start.15
  244.0 2.3 copy-start.18
  244.0 2.3 copy-start.21
  244.0 2.3 copy-start.22
